TPU v7x, 256 devices: a whole 4x4x8 slice. The times are simulated.
256 devices in a mesh: dp: 4 (over x), expert: 32 (over z, y), tensor: 2 (over core).
Axes of the slice: x: 4, y: 4, z: 8, core: 2. Of those that a mesh axis runs over, the one named last changes fastest.
Arguments:
- queries: bfloat16 [8192, 4096], P(('dp', 'expert'), 'tensor'), may hold values from -8 to 8
- fresh_keys: bfloat16 [8192, 512], P(('dp', 'expert'), 'tensor'), may hold values from -6 to 6
- fresh_values: bfloat16 [8192, 512], P(('dp', 'expert'), 'tensor'), may hold values from -6 to 6
- resident_keys: bfloat16 [128, 2048, 512], P(('dp', 'expert'), None, 'tensor'), may hold values from -8 to 8
- resident_values: bfloat16 [128, 2048, 512], P(('dp', 'expert'), None, 'tensor'), may hold values from -6 to 6
- out_weight: bfloat16 [4096, 2048], P('tensor', 'dp'), may hold values from -0.5 to 0.5
- residual: bfloat16 [8192, 2048], P(('dp', 'expert')), may hold values from -23 to 23
- norm_gain: float32 [2048], replicated, may hold values from 0.1 to 1.9
- expert_ids: int32 [8192, 8], P(('dp', 'expert')), may hold values from 0 to 127, all different within a row; in each aligned block of 64 rows (0 to 63, 64 to 127, ...) at most 6 rows name the same one
- gates: float32 [8192, 8], P(('dp', 'expert')), may hold values from 0.05 to 0.5
- w_gate: bfloat16 [128, 2048, 768], P(('dp', 'expert'), None, 'tensor'), may hold values from -0.125 to 0.125
- w_up: bfloat16 [128, 2048, 768], P(('dp', 'expert'), None, 'tensor'), may hold values from -0.125 to 0.125
- w_down: bfloat16 [128, 768, 2048], P(('dp', 'expert'), 'tensor'), may hold values from -0.21875 to 0.21875
Outputs:
- mixed: bfloat16 [8192, 2048], P(('dp', 'expert'), 'tensor')
Inputs may be any that keep to these rules, and one draw needn't show every extreme that they name: `expert_ids`: within the 64 tokens of one sequence no expert is named by more than 6 tokens, a bound that some block reaches; a token names 8 different experts.
All inputs are finite; a program needn't handle non-finite values.
Results may differ from a plain program's by a relative error of at most 0.0085.
Values may be sent and summed in bfloat16 or wider, within the bound.
No kernel may reach another device: no remote copies, remote signals or barrier semaphores. Data moves between devices by JAX's collectives and lax.ppermute only.
A program may use at most 64 MiB of HBM per device.

v0:
```python
import jax
import jax.numpy as jnp
from jax import lax
from jax.sharding import PartitionSpec as P

D = 2048
HEAD_WIDTH = 128


def attend_local(queries, fresh_keys, fresh_values, resident_keys, resident_values):
    tokens_here = queries.shape[0]
    kv_here = fresh_keys.shape[1] // HEAD_WIDTH
    query_group = queries.shape[1] // HEAD_WIDTH // kv_here
    context = resident_keys.shape[1]
    query_rows = queries.reshape(tokens_here, kv_here, query_group, HEAD_WIDTH)
    joined_keys = jnp.concatenate([resident_keys[0], fresh_keys], 0).reshape(
        context + tokens_here, kv_here, HEAD_WIDTH
    )
    joined_values = jnp.concatenate([resident_values[0], fresh_values], 0).reshape(
        context + tokens_here, kv_here, HEAD_WIDTH
    )
    score = jnp.einsum(
        "tjgd,sjd->jgts", query_rows, joined_keys, preferred_element_type=jnp.float32
    ) * HEAD_WIDTH ** (-0.5)
    places = jnp.arange(context + tokens_here)
    rows = jnp.arange(tokens_here)
    allowed = (places[None, :] < context) | (places[None, :] - context <= rows[:, None])
    score = jnp.where(allowed, score, jnp.float32(-1e30))
    top_score = jnp.max(score, axis=-1, keepdims=True)
    weight = jnp.exp(score - top_score)
    probs = (weight / jnp.sum(weight, axis=-1, keepdims=True)).astype(jnp.bfloat16)
    attended = jnp.einsum(
        "jgts,sjd->tjgd", probs, joined_values, preferred_element_type=jnp.float32
    )
    return attended.reshape(tokens_here, -1).astype(jnp.bfloat16)


def expert_rows(block, gate_mat, up_mat, down_mat):
    sources, items, width = block.shape
    flat = block.reshape(sources * items, width)
    gate_part = jnp.dot(flat, gate_mat, preferred_element_type=jnp.float32)
    up_part = jnp.dot(flat, up_mat, preferred_element_type=jnp.float32)
    act = (jax.nn.silu(gate_part) * up_part).astype(jnp.bfloat16)
    result = jnp.dot(act, down_mat, preferred_element_type=jnp.float32)
    return result.reshape(sources, items, -1)


def per_device(
    queries,
    fresh_keys,
    fresh_values,
    resident_keys,
    resident_values,
    out_weight,
    residual,
    norm_gain,
    expert_ids,
    gates,
    w_gate,
    w_up,
    w_down,
):
    attended = attend_local(queries, fresh_keys, fresh_values, resident_keys, resident_values)
    partial_sum = jnp.dot(
        attended,
        lax.all_gather(out_weight, "dp", axis=1, tiled=True),
        preferred_element_type=jnp.float32,
    )
    tokens_here = residual.shape[0]
    pairs = lax.axis_size("tensor")
    half = D // pairs
    lane = lax.axis_index("tensor")
    summed = lax.psum(partial_sum.astype(jnp.bfloat16), "tensor").astype(jnp.float32)
    hidden = residual.astype(jnp.float32) + summed
    mean_square = jnp.mean(hidden * hidden, axis=-1, keepdims=True)
    normed = (hidden * lax.rsqrt(mean_square + 1e-06) * norm_gain).astype(jnp.bfloat16)
    hidden_half = lax.dynamic_slice_in_dim(hidden, lane * half, half, 1)
    owners = lax.axis_size("dp") * lax.axis_size("expert")
    top = expert_ids.shape[1]
    slots = max(2, tokens_here * top * 3 // (2 * owners))
    onehot = (expert_ids[:, :, None] == jnp.arange(owners)[None, None, :]).astype(jnp.int32)
    per_token = jnp.sum(onehot, axis=1)
    before = jnp.cumsum(per_token, axis=0) - per_token
    slot = jnp.sum(onehot * before[:, None, :], axis=-1)
    token_rows = jnp.broadcast_to(
        jnp.arange(tokens_here, dtype=jnp.int32)[:, None], expert_ids.shape
    )
    owner_rows = jnp.full((owners, slots), -1, jnp.int32).at[expert_ids, slot].set(token_rows)
    valid = owner_rows >= 0
    outgoing = jnp.where(
        valid[:, :, None], normed[jnp.maximum(owner_rows, 0)], jnp.zeros((), jnp.bfloat16)
    )
    expert_part = expert_rows(
        lax.all_to_all(outgoing, ("dp", "expert"), split_axis=0, concat_axis=0, tiled=True),
        w_gate[0],
        w_up[0],
        w_down[0],
    )
    owned = lax.psum_scatter(
        expert_part.astype(jnp.bfloat16), "tensor", scatter_dimension=2, tiled=True
    )
    returned = lax.all_to_all(owned, ("dp", "expert"), split_axis=0, concat_axis=0, tiled=True)
    picked = returned[expert_ids, slot]
    moe = jnp.sum(gates[:, :, None] * picked.astype(jnp.float32), axis=1)
    return (hidden_half + moe).astype(jnp.bfloat16)


def solution(mesh):
    return jax.shard_map(
        per_device,
        mesh=mesh,
        in_specs=(
            P(("dp", "expert"), "tensor"),
            P(("dp", "expert"), "tensor"),
            P(("dp", "expert"), "tensor"),
            P(("dp", "expert"), None, "tensor"),
            P(("dp", "expert"), None, "tensor"),
            P("tensor", "dp"),
            P(("dp", "expert"), None),
            P(),
            P(("dp", "expert"), None),
            P(("dp", "expert"), None),
            P(("dp", "expert"), None, "tensor"),
            P(("dp", "expert"), None, "tensor"),
            P(("dp", "expert"), "tensor", None),
        ),
        out_specs=P(("dp", "expert"), "tensor"),
        check_vma=False,
    )
```

profile of v0, /device:TPU:32, one launch (start us, length us, event | category | flops | bytes accessed | tf_op | source)
XLA Modules:
  0.0 379.2 jit_solution(17011101792321861209)
XLA Ops:
  6.5 0.7 all-gather.2.cloned.1.call-update
  7.3 1.5 copy.74
  8.8 1.4 copy.75
  10.3 1.5 copy.71
  11.8 1.3 copy.72
  13.3 4.6 %fusion.46 = f32[2,8,64]{2,1,0:T(8,128)S(1)} fusion(pred[64,2112]{1,0:T(8,128)(4,1)S(1)} %fusion.26, bf16[64,2,128]{2,0,1:T(8,128)(2,1)S(1)} %get-tuple-element.9, bf16[2048,2,128]{2,0,1:T(8,128)(2,1)} %copy.75, bf16[64,2,8,128]{3,2,1,0:T(8,128)(2,1)S(1)} %bitcast.97), kind=kOutput, calls=%fused_computation.69 | convolution fusion | flops 564463680 | bytes 1482752 | tf_op jit(solution)/shard_map/sub | solution.py:30
  17.9 4.9 %fusion.19 = bf16[64,2,8,128]{3,0,2,1:T(8,128)(2,1)S(1)} fusion(f32[2,8,64]{2,1,0:T(8,128)S(1)} %fusion.46, bf16[64,2,128]{2,0,1:T(8,128)(2,1)S(1)} %get-tuple-element.10, bf16[2048,2,128]{2,0,1:T(8,128)(2,1)} %copy.72, pred[64,2112]{1,0:T(8,128)(4,1)S(1)} %fusion.26, bf16[64,2,128]{2,0,1:T(8,128)(2,1)S(1)} %get-tuple-element.9, ...), kind=kOutput, calls=%fused_computation.25 | convolution fusion | flops 1122569216 | bytes 2826240 | tf_op jit(solution)/shard_map/jgts,sjd->tjgd/dot_general | solution.py:32
  23.4 1.2 select_reduce_fusion
  25.0 22.0 %scatter_fusion = s32[128,6]{0,1:T(8,128)S(1)} fusion(s32[128,6]{0,1:T(8,128)S(1)} %broadcast_in_dim.26, s32[512]{0:T(512)S(1)} %reshape.80, s32[512]{0:T(512)S(1)} %reshape.82), kind=kCustom, calls=%fused_computation.2 | custom fusion | bytes 10240 | tf_op jit(solution)/shard_map/scatter | solution.py:88
  47.3 50.1 %all-gather.2.cloned.1.call-done = bf16[2048,2048]{1,0:T(8,128)(2,1)} async-done(((bf16[2048,512]{1,0:T(8,128)(2,1)}), bf16[2048,2048]{1,0:T(8,128)(2,1)}) %all-gather.2.cloned.1.call-update) | async-done | bytes 8388624 | tf_op jit(solution)/shard_map/all_gather | solution.py:66
  97.4 5.7 %convolution_convert_fusion.1 = bf16[64,2048]{1,0:T(8,128)(2,1)} fusion(bf16[2048,2048]{1,0:T(8,128)(2,1)} %all-gather.2.cloned.1.call-done, bf16[8,8,16,128]{3,2,1,0:T(8,128)(2,1)S(1)} %bitcast.95), kind=kOutput, calls=%fused_computation.14 | convolution fusion | flops 537001984 | bytes 8912896 | tf_op jit(solution)/shard_map/dot_general | solution.py:64
  103.1 0.2 reduce-scatter.2.cloned.1.call-start
  103.5 29.8 %all-reduce.2.cloned.1.call-done = bf16[64,2048]{1,0:T(8,128)(2,1)} async-done(((bf16[64,2048]{1,0:T(8,128)(2,1)}), bf16[64,2048]{1,0:T(8,128)(2,1)}) %all-reduce.2.cloned.1.call-update) | async-done | bytes 262160 | tf_op jit(solution)/shard_map/psum | solution.py:73
  133.3 1.9 convert_add_fusion
  135.3 1.1 multiply_convert_fusion
  136.3 4.3 %gather_fusion = bf16[768,2048]{1,0:T(8,128)(2,1)} fusion(bf16[64,2048]{1,0:T(8,128)(2,1)S(1)} %multiply_convert_fusion, s32[1024]{0:T(1024)S(1)} %pad_clamp_fusion), kind=kCustom, calls=%fused_computation | custom fusion | bytes 6294528 | tf_op jit(solution)/shard_map/gather | solution.py:91
  140.6 6.3 %reshape.67 = bf16[128,6,2048]{2,1,0:T(8,128)(2,1)} reshape(bf16[768,2048]{1,0:T(8,128)(2,1)} %gather_fusion) | data formatting | bytes 6291456 | tf_op jit(solution)/shard_map/gather | solution.py:91
  146.9 2.6 broadcast_select_fusion
  149.5 111.2 %all_to_all.10 = bf16[128,6,2048]{2,1,0:T(8,128)(2,1)} all-to-all(bf16[128,6,2048]{2,1,0:T(8,128)(2,1)S(1)} %broadcast_select_fusion), channel_id=1, replica_groups=mesh['dp'=4,'expert'=32,'tensor'=2] {'dp','expert'}, dimensions={0} | all-to-all | bytes 6291456 | tf_op jit(solution)/shard_map/all_to_all | solution.py:94
  260.8 6.3 %reshape.65 = bf16[768,2048]{1,0:T(8,128)(2,1)} reshape(bf16[128,6,2048]{2,1,0:T(8,128)(2,1)} %all_to_all.10) | data formatting | bytes 6291456 | tf_op jit(solution)/shard_map/reshape | solution.py:40
  267.1 4.3 %fusion.10 = f32[768,384]{1,0:T(8,128)S(1)} fusion(bf16[768,2048]{1,0:T(8,128)(2,1)} %reshape.65, bf16[1,2048,384]{2,1,0:T(8,128)(2,1)} %param.23), kind=kOutput, calls=%fused_computation.20 | convolution fusion | flops 1207959552 | bytes 5898240 | tf_op jit(solution)/shard_map/dot_general | solution.py:41
  271.4 1.8 fusion.15
  273.3 0.2 dot_general.25
  273.5 3.5 convolution_convert_fusion
  277.0 11.5 %reduce-scatter.2.cloned.1.call-done = bf16[128,6,1024]{2,0,1:T(8,128)(2,1)} async-done(((bf16[128,6,2048]{2,0,1:T(8,128)(2,1)}), bf16[128,6,1024]{2,0,1:T(8,128)(2,1)}) %reduce-scatter.2.cloned.1.call-update) | async-done | bytes 1572880 | tf_op jit(solution)/shard_map/reduce_scatter | solution.py:99
  288.4 3.6 copy.86
  292.1 14.3 %all-to-all-start.1 = ((bf16[128,6,1024]{2,1,0:T(8,128)(2,1)}), bf16[128,6,1024]{2,1,0:T(8,128)(2,1)}, u32[]{:S(2)}, u32[]{:S(2)}) async-start(bf16[128,6,1024]{2,1,0:T(8,128)(2,1)} %copy.86), calls=%async_computation.2 | async-start | bytes 4194304 | tf_op jit(solution)/shard_map/all_to_all | solution.py:102
  306.7 52.1 %all-to-all-done.1 = bf16[128,6,1024]{2,1,0:T(8,128)(2,1)} async-done(((bf16[128,6,1024]{2,1,0:T(8,128)(2,1)}), bf16[128,6,1024]{2,1,0:T(8,128)(2,1)}, u32[]{:S(2)}, u32[]{:S(2)}) %all-to-all-start.1) | async-done | bytes 1572896 | tf_op jit(solution)/shard_map/all_to_all | solution.py:102
  358.8 2.5 copy.88
  361.2 7.9 %gather_fusion.1 = bf16[512,1024]{1,0:T(8,128)(2,1)} fusion(bf16[128,6,1024]{2,0,1:T(8,128)(2,1)S(1)} %copy.88, s32[512]{0:T(512)S(1)} %reshape.74), kind=kCustom, calls=%fused_computation.1 | custom fusion | bytes 2101248 | tf_op jit(solution)/shard_map/gather | solution.py:103
  369.1 1.9 fusion.6
  371.0 1.6 add_convert_fusion
  (53 shorter events, 1.8 us)
Async XLA Ops:
  6.5 266.9 %copy-start = (bf16[1,384,2048]{2,1,0:T(8,128)(2,1)S(1)}, bf16[1,384,2048]{2,1,0:T(8,128)(2,1)}, u32[]{:S(2)}) copy-start(bf16[1,384,2048]{2,1,0:T(8,128)(2,1)} %param.25) | copy-start | bytes 4718596
  6.5 90.8 %all-gather.2.cloned.1.call-start = ((), (), s32[]{:S(2)}) async-start(), calls=%async_computation.3 | async-start | bytes 10485760 | tf_op jit(solution)/shard_map/all_gather | solution.py:66
  7.3 3.0 copy-start.4
  7.3 126.1 %all-reduce.2.cloned.1.call-start = ((), (), s32[]{:S(2)}) async-start(), calls=%async_computation.4 | async-start | bytes 524288 | tf_op jit(solution)/shard_map/psum | solution.py:73
  10.3 2.8 copy-start.5
  10.3 2.8 copy-start.6
  13.3 4.7 %copy-start.2 = (bf16[2048,2,128]{2,0,1:T(8,128)(2,1)S(1)}, bf16[2048,2,128]{2,0,1:T(8,128)(2,1)}, u32[]{:S(2)}) copy-start(bf16[2048,2,128]{2,0,1:T(8,128)(2,1)} %copy.75) | copy-start | bytes 3145732
  17.9 5.1 %copy-start.7 = (s32[64,8]{0,1:T(8,128)S(1)}, s32[64,8]{0,1:T(8,128)}, u32[]{:S(2)}) copy-start(s32[64,8]{0,1:T(8,128)} %param.21) | copy-start | bytes 6148
  97.4 35.9 %copy-start.3 = (bf16[64,2048]{1,0:T(8,128)(2,1)S(1)}, bf16[64,2048]{1,0:T(8,128)(2,1)}, u32[]{:S(2)}) copy-start(bf16[64,2048]{1,0:T(8,128)(2,1)} %param.19) | copy-start | bytes 786436
  97.4 37.9 %copy-start.8 = (f32[2048]{0:T(1024)S(1)}, f32[2048]{0:T(1024)}, u32[]{:S(2)}) copy-start(f32[2048]{0:T(1024)} %param.20) | copy-start | bytes 24580
  103.1 185.3 %reduce-scatter.2.cloned.1.call-start = ((), (), s32[]{:S(2)}) async-start(), calls=%async_computation.5 | async-start | bytes 4718592 | tf_op jit(solution)/shard_map/reduce_scatter | solution.py:99
  267.1 4.3 %copy-start.1 = (bf16[768,2048]{1,0:T(8,128)(2,1)S(1)}, bf16[768,2048]{1,0:T(8,128)(2,1)}, u32[]{:S(2)}) copy-start(bf16[768,2048]{1,0:T(8,128)(2,1)} %reshape.65) | copy-start | bytes 9437188
  267.1 4.3 %copy-start.10 = (bf16[1,2048,384]{2,1,0:T(8,128)(2,1)S(1)}, bf16[1,2048,384]{2,1,0:T(8,128)(2,1)}, u32[]{:S(2)}) copy-start(bf16[1,2048,384]{2,1,0:T(8,128)(2,1)} %param.24) | copy-start | bytes 4718596
  292.1 14.5 %copy-start.9 = (f32[64,8]{0,1:T(8,128)S(1)}, f32[64,8]{0,1:T(8,128)}, u32[]{:S(2)}) copy-start(f32[64,8]{0,1:T(8,128)} %param.22) | copy-start | bytes 6148
  292.1 66.7 %all-to-all-start.1 = ((bf16[128,6,1024]{2,1,0:T(8,128)(2,1)}), bf16[128,6,1024]{2,1,0:T(8,128)(2,1)}, u32[]{:S(2)}, u32[]{:S(2)}) async-start(bf16[128,6,1024]{2,1,0:T(8,128)(2,1)} %copy.86), calls=%async_computation.2 | async-start | bytes 4194304 | tf_op jit(solution)/shard_map/all_to_all | solution.py:102
Sparse Core Ops, SparseCore 0:
  9.1 88.1 all-gather.1
  103.2 30.0 all-reduce.1
  277.1 11.3 reduce-scatter.1
where the time goes:
time: 380 us; the launch traced here: 379 us
  waiting for transfers between devices  144 us (38%)
  blocking collectives  111 us (29%)
  local copies, waits for them, and re-layouts  60 us (16%)
  matrix products  24.9 us (7%)
  starting transfers between devices  14.6 us (4%)
  between operations  13.4 us (4%)
  other arithmetic  10.8 us (3%)
    all_to_all x1, blocking collectives, per_device(): lax.all_to_all(outgoing, ('dp', 'expert'), split_axis=0, concat_axis=0, t...  111 us
    all_to_all x1, waiting for transfers between devices, per_device(): lax.all_to_all(owned, ('dp', 'expert'), split_axis=0, concat_axis=0, tile...  52.1 us
    all_gather x1, waiting for transfers between devices, per_device(): lax.all_gather(out_weight, 'dp', axis=1, tiled=True)  50.1 us
    psum x1, waiting for transfers between devices, per_device(): lax.psum(partial_sum.astype(jnp.bfloat16), 'tensor').astype(jnp.float32)  29.8 us
    scatter x1, local copies, waits for them, and re-layouts, per_device(): jnp.full((owners, slots), -1, jnp.int32).at[expert_ids, slot]  22 us
    all_to_all x1, starting transfers between devices, per_device(): lax.all_to_all(owned, ('dp', 'expert'), split_axis=0, concat_axis=0, tile...  14.3 us
    reduce_scatter x1, waiting for transfers between devices, per_device(): lax.psum_scatter(expert_part.astype(jnp.bfloat16), 'tensor', scatter_dime...  11.5 us
    gather x2, local copies, waits for them, and re-layouts, per_device(): normed[jnp.maximum(owner_rows, 0)]  10.5 us
  transfers between devices with their start and end apart: 4, of which 4 were waited for; matrix products, arithmetic and copies ran while one was open for 11% of the time, Pallas kernels for 0%

commit v1 on v0

--- a/solution.py
+++ b/solution.py
@@ -2,9 +2,15 @@
 import jax.numpy as jnp
 from jax import lax
 from jax.sharding import PartitionSpec as P
+from jax.lax import all_gather
 
 D = 2048
 HEAD_WIDTH = 128
+
+
+def time_inputs(vec, named_axis):
+    y_new = all_gather(vec, named_axis).sum(axis=0)
+    return y_new
 
 
 def attend_local(queries, fresh_keys, fresh_values, resident_keys, resident_values):
@@ -70,7 +76,7 @@
     pairs = lax.axis_size("tensor")
     half = D // pairs
     lane = lax.axis_index("tensor")
-    summed = lax.psum(partial_sum.astype(jnp.bfloat16), "tensor").astype(jnp.float32)
+    summed = time_inputs(partial_sum.astype(jnp.bfloat16), named_axis="tensor").astype(jnp.float32)
     hidden = residual.astype(jnp.float32) + summed
     mean_square = jnp.mean(hidden * hidden, axis=-1, keepdims=True)
     normed = (hidden * lax.rsqrt(mean_square + 1e-06) * norm_gain).astype(jnp.bfloat16)

time: 380 us -> 349 us (0.918)
  waiting for transfers between devices: 144 us -> 114 us
    psum x1 -> x0, waiting for transfers between devices: 29.8 us -> none  [per_device(): lax.psum(partial_sum.astype(jnp.bfloat16), 'tensor').astype(jnp.float32)]
  transfers between devices with their start and end apart: 4 -> 3, of which waited for: 4 -> 3; matrix products, arithmetic and copies ran while one was open for 11% -> 12% of each run, Pallas kernels for 0% -> 0%
where the time goes in v1:
time: 349 us
  waiting for transfers between devices  114 us (33%)
  blocking collectives  113 us (32%)
  local copies, waits for them, and re-layouts  60 us (17%)
  matrix products  24.2 us (7%)
  starting transfers between devices  14.3 us (4%)
  between operations  13.7 us (4%)
  other arithmetic  9.05 us (3%)
    all_to_all x1, blocking collectives, per_device(): lax.all_to_all(outgoing, ('dp', 'expert'), split_axis=0, concat_axis=0, t...  111 us
    all_to_all x1, waiting for transfers between devices, per_device(): lax.all_to_all(owned, ('dp', 'expert'), split_axis=0, concat_axis=0, tile...  52.1 us
    all_gather x1, waiting for transfers between devices, per_device(): lax.all_gather(out_weight, 'dp', axis=1, tiled=True)  50 us
    scatter x1, local copies, waits for them, and re-layouts, per_device(): jnp.full((owners, slots), -1, jnp.int32).at[expert_ids, slot]  22 us
    all_to_all x1, starting transfers between devices, per_device(): lax.all_to_all(owned, ('dp', 'expert'), split_axis=0, concat_axis=0, tile...  14.3 us
    reduce_scatter x1, waiting for transfers between devices, per_device(): lax.psum_scatter(expert_part.astype(jnp.bfloat16), 'tensor', scatter_dime...  11.4 us
    gather x2, local copies, waits for them, and re-layouts, per_device(): normed[jnp.maximum(owner_rows, 0)]  10.5 us
    gather x1, local copies, waits for them, and re-layouts, per_device(): picked = returned[expert_ids, slot]  7.86 us
  transfers between devices with their start and end apart: 3, of which 3 were waited for; matrix products, arithmetic and copies ran while one was open for 12% of the time, Pallas kernels for 0%

profile of v1, /device:TPU:32, one launch (start us, length us, event | category | flops | bytes accessed | tf_op | source)
XLA Modules:
  0.0 348.7 jit_solution(3028531344032417523)
XLA Ops:
  6.5 0.7 all-gather.3.cloned.1.call-update
  7.3 1.5 copy.74
  8.8 1.4 copy.75
  10.3 1.5 copy.71
  11.8 1.3 copy.72
  13.3 4.6 %fusion.46 = f32[2,8,64]{2,1,0:T(8,128)S(1)} fusion(pred[64,2112]{1,0:T(8,128)(4,1)S(1)} %fusion.26, bf16[64,2,128]{2,0,1:T(8,128)(2,1)S(1)} %get-tuple-element.9, bf16[2048,2,128]{2,0,1:T(8,128)(2,1)} %copy.75, bf16[64,2,8,128]{3,2,1,0:T(8,128)(2,1)S(1)} %bitcast.99), kind=kOutput, calls=%fused_computation.69 | convolution fusion | flops 564463680 | bytes 1482752 | tf_op jit(solution)/shard_map/sub | solution.py:36
  17.9 4.9 %fusion.19 = bf16[64,2,8,128]{3,0,2,1:T(8,128)(2,1)S(1)} fusion(f32[2,8,64]{2,1,0:T(8,128)S(1)} %fusion.46, bf16[64,2,128]{2,0,1:T(8,128)(2,1)S(1)} %get-tuple-element.10, bf16[2048,2,128]{2,0,1:T(8,128)(2,1)} %copy.72, pred[64,2112]{1,0:T(8,128)(4,1)S(1)} %fusion.26, bf16[64,2,128]{2,0,1:T(8,128)(2,1)S(1)} %get-tuple-element.9, ...), kind=kOutput, calls=%fused_computation.25 | convolution fusion | flops 1122569216 | bytes 2826240 | tf_op jit(solution)/shard_map/jgts,sjd->tjgd/dot_general | solution.py:38
  22.8 0.2 copy.78
  23.1 0.1 convert_reduce_fusion
  23.4 1.2 select_reduce_fusion
  25.0 22.0 %scatter_fusion = s32[128,6]{0,1:T(8,128)S(1)} fusion(s32[128,6]{0,1:T(8,128)S(1)} %broadcast_in_dim.26, s32[512]{0:T(512)S(1)} %reshape.80, s32[512]{0:T(512)S(1)} %reshape.82), kind=kCustom, calls=%fused_computation.2 | custom fusion | bytes 10240 | tf_op jit(solution)/shard_map/scatter | solution.py:94
  47.4 50.0 %all-gather.3.cloned.1.call-done = bf16[2048,2048]{1,0:T(8,128)(2,1)} async-done(((bf16[2048,512]{1,0:T(8,128)(2,1)}), bf16[2048,2048]{1,0:T(8,128)(2,1)}) %all-gather.3.cloned.1.call-update) | async-done | bytes 8388624 | tf_op jit(solution)/shard_map/all_gather | solution.py:72
  97.4 5.0 %convolution_convert_fusion.1 = bf16[64,2048]{1,0:T(8,128)(2,1)S(1)} fusion(bf16[2048,2048]{1,0:T(8,128)(2,1)} %all-gather.3.cloned.1.call-done, bf16[8,8,16,128]{3,2,1,0:T(8,128)(2,1)S(1)} %bitcast.96), kind=kOutput, calls=%fused_computation.14 | convolution fusion | flops 537001984 | bytes 8912896 | tf_op jit(solution)/shard_map/dot_general | solution.py:70
  102.4 2.4 all-gather
  104.9 1.0 convert_add_fusion
  106.0 4.3 %gather_fusion = bf16[768,2048]{1,0:T(8,128)(2,1)} fusion(bf16[64,2048]{1,0:T(8,128)(2,1)S(1)} %multiply_convert_fusion, s32[1024]{0:T(1024)S(1)} %pad_clamp_fusion), kind=kCustom, calls=%fused_computation | custom fusion | bytes 6294528 | tf_op jit(solution)/shard_map/gather | solution.py:97
  110.3 6.3 %reshape.67 = bf16[128,6,2048]{2,1,0:T(8,128)(2,1)} reshape(bf16[768,2048]{1,0:T(8,128)(2,1)} %gather_fusion) | data formatting | bytes 6291456 | tf_op jit(solution)/shard_map/gather | solution.py:97
  116.5 2.6 broadcast_select_fusion
  119.2 110.9 %all_to_all.10 = bf16[128,6,2048]{2,1,0:T(8,128)(2,1)} all-to-all(bf16[128,6,2048]{2,1,0:T(8,128)(2,1)S(1)} %broadcast_select_fusion), channel_id=1, replica_groups=mesh['dp'=4,'expert'=32,'tensor'=2] {'dp','expert'}, dimensions={0} | all-to-all | bytes 6291456 | tf_op jit(solution)/shard_map/all_to_all | solution.py:100
  230.1 6.3 %reshape.65 = bf16[768,2048]{1,0:T(8,128)(2,1)} reshape(bf16[128,6,2048]{2,1,0:T(8,128)(2,1)} %all_to_all.10) | data formatting | bytes 6291456 | tf_op jit(solution)/shard_map/reshape | solution.py:46
  236.4 4.3 %fusion.10 = f32[768,384]{1,0:T(8,128)S(1)} fusion(bf16[768,2048]{1,0:T(8,128)(2,1)} %reshape.65, bf16[1,2048,384]{2,1,0:T(8,128)(2,1)} %param.23), kind=kOutput, calls=%fused_computation.20 | convolution fusion | flops 1207959552 | bytes 5898240 | tf_op jit(solution)/shard_map/dot_general | solution.py:47
  240.7 1.8 fusion.15
  242.6 0.2 dot_general.25
  242.8 3.5 convolution_convert_fusion
  246.3 11.4 %reduce-scatter.2.cloned.1.call-done = bf16[128,6,1024]{2,0,1:T(8,128)(2,1)} async-done(((bf16[128,6,2048]{2,0,1:T(8,128)(2,1)}), bf16[128,6,1024]{2,0,1:T(8,128)(2,1)}) %reduce-scatter.2.cloned.1.call-update) | async-done | bytes 1572880 | tf_op jit(solution)/shard_map/reduce_scatter | solution.py:105
  257.7 3.6 %copy.86 = bf16[128,6,1024]{2,1,0:T(8,128)(2,1)} copy(bf16[128,6,1024]{2,0,1:T(8,128)(2,1)} %reduce-scatter.2.cloned.1.call-done) | data formatting | bytes 3145728 | tf_op jit(solution)/shard_map/reduce_scatter | solution.py:105
  261.3 14.3 %all-to-all-start.1 = ((bf16[128,6,1024]{2,1,0:T(8,128)(2,1)}), bf16[128,6,1024]{2,1,0:T(8,128)(2,1)}, u32[]{:S(2)}, u32[]{:S(2)}) async-start(bf16[128,6,1024]{2,1,0:T(8,128)(2,1)} %copy.86), calls=%async_computation.2 | async-start | bytes 4194304 | tf_op jit(solution)/shard_map/all_to_all | solution.py:108
  275.9 52.1 %all-to-all-done.1 = bf16[128,6,1024]{2,1,0:T(8,128)(2,1)} async-done(((bf16[128,6,1024]{2,1,0:T(8,128)(2,1)}), bf16[128,6,1024]{2,1,0:T(8,128)(2,1)}, u32[]{:S(2)}, u32[]{:S(2)}) %all-to-all-start.1) | async-done | bytes 1572896 | tf_op jit(solution)/shard_map/all_to_all | solution.py:108
  328.0 2.5 copy.88
  330.4 7.9 %gather_fusion.1 = bf16[512,1024]{1,0:T(8,128)(2,1)} fusion(bf16[128,6,1024]{2,0,1:T(8,128)(2,1)S(1)} %copy.88, s32[512]{0:T(512)S(1)} %reshape.74), kind=kCustom, calls=%fused_computation.1 | custom fusion | bytes 2101248 | tf_op jit(solution)/shard_map/gather | solution.py:109
  338.3 1.9 fusion.6
  340.2 1.6 add_convert_fusion
  (52 shorter events, 1.7 us)
Async XLA Ops:
  6.5 236.2 %copy-start = (bf16[1,384,2048]{2,1,0:T(8,128)(2,1)S(1)}, bf16[1,384,2048]{2,1,0:T(8,128)(2,1)}, u32[]{:S(2)}) copy-start(bf16[1,384,2048]{2,1,0:T(8,128)(2,1)} %param.25) | copy-start | bytes 4718596
  6.5 90.8 %all-gather.3.cloned.1.call-start = ((), (), s32[]{:S(2)}) async-start(), calls=%async_computation.3 | async-start | bytes 10485760 | tf_op jit(solution)/shard_map/all_gather | solution.py:72
  7.3 3.0 copy-start.4
  7.3 250.4 %reduce-scatter.2.cloned.1.call-start = ((), (), s32[]{:S(2)}) async-start(), calls=%async_computation.4 | async-start | bytes 4718592 | tf_op jit(solution)/shard_map/reduce_scatter | solution.py:105
  10.3 2.8 copy-start.5
  10.3 2.8 copy-start.6
  13.3 4.7 %copy-start.2 = (bf16[2048,2,128]{2,0,1:T(8,128)(2,1)S(1)}, bf16[2048,2,128]{2,0,1:T(8,128)(2,1)}, u32[]{:S(2)}) copy-start(bf16[2048,2,128]{2,0,1:T(8,128)(2,1)} %copy.75) | copy-start | bytes 3145732
  17.9 5.1 %copy-start.7 = (s32[64,8]{0,1:T(8,128)S(1)}, s32[64,8]{0,1:T(8,128)}, u32[]{:S(2)}) copy-start(s32[64,8]{0,1:T(8,128)} %param.21) | copy-start | bytes 6148
  97.4 7.5 %copy-start.3 = (bf16[64,2048]{1,0:T(8,128)(2,1)S(1)}, bf16[64,2048]{1,0:T(8,128)(2,1)}, u32[]{:S(2)}) copy-start(bf16[64,2048]{1,0:T(8,128)(2,1)} %param.19) | copy-start | bytes 786436
  102.4 3.5 %copy-start.8 = (f32[2048]{0:T(1024)S(1)}, f32[2048]{0:T(1024)}, u32[]{:S(2)}) copy-start(f32[2048]{0:T(1024)} %param.20) | copy-start | bytes 24580
  236.4 4.3 %copy-start.1 = (bf16[768,2048]{1,0:T(8,128)(2,1)S(1)}, bf16[768,2048]{1,0:T(8,128)(2,1)}, u32[]{:S(2)}) copy-start(bf16[768,2048]{1,0:T(8,128)(2,1)} %reshape.65) | copy-start | bytes 9437188
  236.4 4.3 %copy-start.10 = (bf16[1,2048,384]{2,1,0:T(8,128)(2,1)S(1)}, bf16[1,2048,384]{2,1,0:T(8,128)(2,1)}, u32[]{:S(2)}) copy-start(bf16[1,2048,384]{2,1,0:T(8,128)(2,1)} %param.24) | copy-start | bytes 4718596
  261.3 14.5 %copy-start.9 = (f32[64,8]{0,1:T(8,128)S(1)}, f32[64,8]{0,1:T(8,128)}, u32[]{:S(2)}) copy-start(f32[64,8]{0,1:T(8,128)} %param.22) | copy-start | bytes 6148
  261.3 66.6 %all-to-all-start.1 = ((bf16[128,6,1024]{2,1,0:T(8,128)(2,1)}), bf16[128,6,1024]{2,1,0:T(8,128)(2,1)}, u32[]{:S(2)}, u32[]{:S(2)}) async-start(bf16[128,6,1024]{2,1,0:T(8,128)(2,1)} %copy.86), calls=%async_computation.2 | async-start | bytes 4194304 | tf_op jit(solution)/shard_map/all_to_all | solution.py:108
Sparse Core Ops, SparseCore 0:
  9.1 88.1 all-gather.2
  246.4 11.2 reduce-scatter.1
